TPU v7x, 512 devices: a whole 4x8x8 slice. The times are simulated.
512 devices in a mesh: rows: 32 (over z, x), seq: 16 (over y, core).
Axes of the slice: x: 4, y: 8, z: 8, core: 2. Of those that a mesh axis runs over, the one named last changes fastest.
Arguments:
- qkv: bfloat16 [32, 1024, 3840], P('rows', 'seq'), may hold values from -24 to 24
- hidden: bfloat16 [32, 1024, 1280], P('rows', 'seq'), may hold values from -3 to 3
- segment_ids: int32 [32, 1024], P('rows', 'seq'), may hold values from 0 to 4, as said below
- key_keep: int32 [32, 1024], P('rows', 'seq'), may hold values 0 or 1
- grid_sizes: int32 [32, 4, 2], P('rows'), may hold values from 8 to 16, as said below
- owner_slots: int32 [32, 4], P('rows'), may hold values from 0 to 15, as said below
- out_weight: bfloat16 [1280, 1280], P('rows'), may hold values from -0.15625 to 0.15625
- norm_gain: float32 [1280], replicated, may hold values from 0.5 to 1.5
- norm_bias: float32 [1280], replicated, may hold values from -1.5 to 1.5
- merge_weight: bfloat16 [5120, 4096], P(None, 'seq'), may hold values from -0.078125 to 0.078125
Outputs:
- normed: bfloat16 [32, 1024, 1280], P('rows', 'seq')
- request_norm: float32 [32, 16], P('rows', 'seq')
- request_peak: float32 [32, 16], P('rows', 'seq')
Inputs may be any that keep to these rules, and one draw needn't show every extreme that they name: `segment_ids`: segment ids never fall along a pack: image j covers h_j w_j tokens right after image j - 1, and tokens after the last image carry 4; every pack ends with some such padding. Inside an image each aligned group of 4 tokens is one 2 x 2 block of the patch grid, blocks in row-major order. `grid_sizes`: both sides are even; rows run from 8 to 16, columns from 8 to 14; the first image of every pack has 16 rows and 14 columns; the images of a pack agree with segment_ids. `owner_slots`: the images of one pack have distinct slots.
All inputs are finite; a program needn't handle non-finite values. No bound on the sum of `key_keep` on one device may be relied on, other than what follows from the above.
Results may differ from a plain program's by a relative error of at most 0.0057.
Values may be sent and summed in bfloat16 or wider, within the bound.
No kernel may reach another device: no remote copies, remote signals or barrier semaphores. Data moves between devices by JAX's collectives and lax.ppermute only.
A program may use at most 64 MiB of HBM per device.

v0:
```python
import jax
import jax.numpy as jnp
from jax import lax
from jax.sharding import PartitionSpec as P

HEADS = 16
HD = 80
OUT = 4096
SLOT_DEV = 1


def positions(segment, places, patch_grid):
    image_count = patch_grid.shape[0]
    widths = patch_grid[:, 1]
    lengths = patch_grid[:, 0] * widths
    starts = jnp.cumsum(lengths) - lengths
    is_valid = segment < image_count
    image_hot = segment[:, None] == jnp.arange(image_count, dtype=jnp.int32)[None, :]
    begins = jnp.sum(jnp.where(image_hot, starts[None, :], 0), axis=1)
    token_width = jnp.maximum(jnp.sum(jnp.where(image_hot, widths[None, :], 0), axis=1), 2)
    offset = places - begins
    square = offset // 4
    corner = offset % 4
    half_width = token_width // 2
    row_pos = 2 * (square // half_width) + corner // 2
    col_pos = 2 * (square % half_width) + corner % 2
    row_pos = jnp.where(is_valid, row_pos, 0)
    col_pos = jnp.where(is_valid, col_pos, 0)
    return (row_pos, col_pos)


def rotary(values, row_pos, col_pos):
    quarter = values.shape[-1] // 4
    rates = 10000.0 ** (-jnp.arange(quarter, dtype=jnp.float32) / quarter)

    def rotate_pair(part, place):
        angle = place.astype(jnp.float32)[:, None] * rates[None, :]
        cosine = jnp.cos(angle)[:, None, :]
        sine = jnp.sin(angle)[:, None, :]
        first_half = part[..., :quarter]
        second_half = part[..., quarter:]
        return jnp.concatenate(
            [first_half * cosine - second_half * sine, second_half * cosine + first_half * sine],
            axis=-1,
        )

    middle = 2 * quarter
    return jnp.concatenate(
        [rotate_pair(values[..., :middle], row_pos), rotate_pair(values[..., middle:], col_pos)],
        axis=-1,
    )


def layer_norm(mixed, norm_gain, norm_bias):
    row_mean = jnp.mean(mixed, axis=-1, keepdims=True)
    centred = mixed - row_mean
    spread = jnp.mean(centred * centred, axis=-1, keepdims=True)
    return (centred * lax.rsqrt(spread + 1e-05) * norm_gain + norm_bias).astype(jnp.bfloat16)


def slot_counts(patch_grid, owner, slot_total):
    quads = patch_grid[:, 0] * patch_grid[:, 1] // 4
    owner_hot = owner[:, None] == jnp.arange(slot_total, dtype=jnp.int32)[None, :]
    return jnp.sum(jnp.where(owner_hot, quads[:, None], 0), axis=0)


def block_mask(segment_query, segment_keys, keep_keys, query_index, key_index, image_count):
    same_image = (
        (segment_query[:, None] == segment_keys[None, :])
        & (segment_query[:, None] < image_count)
        & (keep_keys[None, :] == 1)
    )
    return same_image | (query_index[:, None] == key_index[None, :])


def attend_dense(queries, key_rows, value_rows, segment_row, keep_row, block_rows, image_count):
    total_rows = queries.shape[1]
    key_index = jnp.arange(total_rows, dtype=jnp.int32)

    def query_block(start):
        query_part = lax.dynamic_slice_in_dim(queries, start, block_rows, 1)
        segment_part = lax.dynamic_slice_in_dim(segment_row, start, block_rows, 0)
        query_index = start + jnp.arange(block_rows, dtype=jnp.int32)
        scores = jnp.einsum(
            "hqd,hkd->hqk", query_part, key_rows, preferred_element_type=jnp.float32
        ) * HD ** (-0.5)
        allowed = block_mask(
            segment_part, segment_row, keep_row, query_index, key_index, image_count
        )[None]
        top = jnp.max(jnp.where(allowed, scores, -1e30), axis=-1, keepdims=True)
        weights = jnp.where(allowed, jnp.exp(scores - top), 0.0)
        totals = jnp.sum(weights, axis=-1, keepdims=True)
        summed = jnp.einsum(
            "hqk,hkd->hqd",
            weights.astype(jnp.bfloat16),
            value_rows,
            preferred_element_type=jnp.float32,
        )
        return (summed / totals).astype(jnp.bfloat16)

    starts = jnp.arange(total_rows // block_rows, dtype=jnp.int32) * block_rows
    blocks_out = lax.map(query_block, starts)
    return jnp.transpose(blocks_out, (1, 0, 2, 3)).reshape(queries.shape)


def body(
    qkv,
    hidden,
    segment_ids,
    key_keep,
    grid_sizes,
    owner_slots,
    out_weight,
    norm_gain,
    norm_bias,
    merge_weight,
):
    seq_count = lax.axis_size("seq")
    tok_count = qkv.shape[1]
    seq_len = tok_count * seq_count
    patch_grid = grid_sizes[0]
    image_count = patch_grid.shape[0]
    owner = owner_slots[0]
    segment = segment_ids[0]
    key_flags = key_keep[0]
    my_index = lax.axis_index("seq")
    first_token = my_index * tok_count
    places = first_token + jnp.arange(tok_count, dtype=jnp.int32)
    row_pos, col_pos = positions(segment, places, patch_grid)
    split = qkv[0].reshape(tok_count, 3, HEADS, HD)
    queries = rotary(split[:, 0].astype(jnp.float32), row_pos, col_pos).astype(jnp.bfloat16)
    key_rows = rotary(split[:, 1].astype(jnp.float32), row_pos, col_pos).astype(jnp.bfloat16)
    head_share = HEADS // seq_count
    packed = jnp.stack([queries, key_rows, split[:, 2]], axis=1).reshape(
        tok_count, 3, seq_count, head_share, HD
    )
    segment_tile = jnp.broadcast_to(
        segment[:, None, None, None, None], (tok_count, 1, seq_count, head_share, 1)
    )
    keep_tile = jnp.broadcast_to(
        key_flags[:, None, None, None, None], (tok_count, 1, seq_count, head_share, 1)
    )
    block_rows = 512
    while seq_len % block_rows:
        block_rows = block_rows // 2
    tile_rows = 128
    while seq_len % tile_rows:
        tile_rows = tile_rows // 2
    packed_all = lax.all_to_all(packed, "seq", split_axis=2, concat_axis=0, tiled=True)
    segment_all = lax.all_to_all(segment_tile, "seq", split_axis=2, concat_axis=0, tiled=True)
    keep_all = lax.all_to_all(keep_tile, "seq", split_axis=2, concat_axis=0, tiled=True)
    segment_row = segment_all[:, 0, 0, 0, 0]
    keep_row = keep_all[:, 0, 0, 0, 0]
    head_queries = jnp.transpose(packed_all[:, 0, 0], (1, 0, 2))
    head_keys = jnp.transpose(packed_all[:, 1, 0], (1, 0, 2))
    head_values = jnp.transpose(packed_all[:, 2, 0], (1, 0, 2))
    result = attend_dense(
        head_queries, head_keys, head_values, segment_row, keep_row, block_rows, image_count
    )
    head_out = jnp.transpose(result, (1, 0, 2))
    token_out = lax.all_to_all(head_out, "seq", split_axis=0, concat_axis=1, tiled=True)
    attended = token_out.reshape(tok_count, HEADS * HD)
    mixed_part = jnp.dot(
        attended,
        lax.all_gather(out_weight, "rows", axis=0, tiled=True),
        preferred_element_type=jnp.float32,
    )
    mixed = hidden[0].astype(jnp.float32) + mixed_part
    normed = layer_norm(mixed, norm_gain, norm_bias)
    merged = normed.reshape(tok_count // 4, 4 * normed.shape[1])
    projected = jnp.dot(
        lax.all_gather(merged, "seq", axis=0, tiled=True),
        merge_weight,
        preferred_element_type=jnp.float32,
    )
    merge_stats = jnp.stack([jnp.sum(projected * projected, axis=1), jnp.max(projected, axis=1)])
    slot_total = SLOT_DEV * seq_count
    lengths = patch_grid[:, 0] * patch_grid[:, 1]
    ends = jnp.cumsum(lengths)
    merge_first = 4 * jnp.arange(seq_len // 4, dtype=jnp.int32)
    merge_image = jnp.sum((merge_first[:, None] >= ends[None, :]).astype(jnp.int32), axis=1)
    is_valid = merge_image < image_count
    image_hot = merge_image[:, None] == jnp.arange(image_count, dtype=jnp.int32)[None, :]
    merge_slot = jnp.sum(jnp.where(image_hot, owner[None, :], 0), axis=1)
    slot_hot = (merge_slot[:, None] == jnp.arange(slot_total, dtype=jnp.int32)[None, :]) & is_valid[
        :, None
    ]
    sums_all = jnp.sum(jnp.where(slot_hot, merge_stats[0][:, None], 0.0), axis=0)
    tops_all = jnp.max(jnp.where(slot_hot, merge_stats[1][:, None], -1e30), axis=0)
    own_first = my_index * SLOT_DEV
    slot_sums = lax.psum_scatter(sums_all, "seq", scatter_dimension=0, tiled=True)
    slot_tops = lax.dynamic_slice_in_dim(lax.pmax(tops_all, "seq"), own_first, SLOT_DEV)
    counts = lax.dynamic_slice_in_dim(
        slot_counts(patch_grid, owner, slot_total), own_first, SLOT_DEV
    )
    present = counts > 0
    divisor = (jnp.maximum(counts, 1) * OUT).astype(jnp.float32)
    norm_out = jnp.where(present, jnp.sqrt(slot_sums / divisor + 1e-06), 0.0)
    peak_out = jnp.where(present, slot_tops, 0.0)
    return (normed[None], norm_out[None], peak_out[None])


def solution(mesh):
    placed = (
        P("rows", "seq", None),
        P("rows", "seq", None),
        P("rows", "seq"),
        P("rows", "seq"),
        P("rows", None, None),
        P("rows", None),
        P("rows", None),
        P(),
        P(),
        P(None, "seq"),
    )
    return jax.shard_map(
        body,
        mesh=mesh,
        in_specs=placed,
        out_specs=(P("rows", "seq", None), P("rows", "seq"), P("rows", "seq")),
        check_vma=False,
    )
```

profile of v0, /device:TPU:1, one launch (start us, length us, event | category | flops | bytes accessed | tf_op | source)
XLA Modules:
  0.0 224.3 jit_solution(8085196978204176360)
XLA Ops:
  7.2 1.4 broadcast_in_dim.146
  8.6 10.1 %all-to-all-start = ((s32[64,1,16,1,1]{0,4,3,1,2:T(1,128)}), s32[64,1,16,1,1]{0,4,3,1,2:T(1,128)S(1)}, u32[]{:S(2)}, u32[]{:S(2)}) async-start(s32[64,1,16,1,1]{0,4,3,1,2:T(1,128)} %broadcast_in_dim.146), calls=%async_computation | async-start | bytes 16384 | tf_op jit(solution)/shard_map/all_to_all | solution.py:150
  19.4 2.4 %reshape_squeeze.3 = bf16[64,3,16,80]{3,2,1,0:T(8,128)(2,1)S(1)} reshape(bf16[1,64,3840]{2,1,0:T(8,128)(2,1)} %param.12) | data formatting | bytes 983040 | tf_op jit(solution)/shard_map/reshape;squeeze | solution.py:130
  30.8 7.3 %all-to-all-start.1 = ((s32[64,1,16,1,1]{0,4,3,1,2:T(1,128)}), s32[64,1,16,1,1]{0,4,3,1,2:T(1,128)S(1)}, u32[]{:S(2)}, u32[]{:S(2)}) async-start(s32[64,1,16,1,1]{0,4,3,1,2:T(1,128)} %broadcast_in_dim.148), calls=%async_computation.1 | async-start | bytes 16384 | tf_op jit(solution)/shard_map/all_to_all | solution.py:151
  38.1 1.5 maximum_bitcast_fusion
  40.7 4.3 %all-to-all-done.1 = s32[64,1,16,1,1]{0,4,3,1,2:T(1,128)S(1)} async-done(((s32[64,1,16,1,1]{0,4,3,1,2:T(1,128)}), s32[64,1,16,1,1]{0,4,3,1,2:T(1,128)S(1)}, u32[]{:S(2)}, u32[]{:S(2)}) %all-to-all-start.1) | async-done | bytes 4128 | tf_op jit(solution)/shard_map/all_to_all | solution.py:151
  45.0 4.1 %all-to-all-start.2 = ((bf16[64,3,16,1,80]{4,0,1,3,2:T(8,128)(2,1)}), bf16[64,3,16,1,80]{4,0,1,3,2:T(8,128)(2,1)S(1)}, u32[]{:S(2)}, u32[]{:S(2)}) async-start(bf16[64,3,16,1,80]{4,0,1,3,2:T(8,128)(2,1)} %copy.49), calls=%async_computation.2 | async-start | bytes 1572864 | tf_op jit(solution)/shard_map/all_to_all | solution.py:149
  49.9 22.0 %all-to-all-done.2 = bf16[64,3,16,1,80]{4,0,1,3,2:T(8,128)(2,1)S(1)} async-done(((bf16[64,3,16,1,80]{4,0,1,3,2:T(8,128)(2,1)}), bf16[64,3,16,1,80]{4,0,1,3,2:T(8,128)(2,1)S(1)}, u32[]{:S(2)}, u32[]{:S(2)}) %all-to-all-start.2) | async-done | bytes 491552 | tf_op jit(solution)/shard_map/all_to_all | solution.py:149
  71.9 1.4 copy.50
  73.3 1.9 all_to_all.61
  76.2 20.3 %while.11 = (s32[]{:T(128)}, bf16[2,1,512,80]{2,3,1,0:T(8,128)(2,1)}, s32[2]{0:T(128)}, s32[1024]{0:T(1024)S(1)}, s32[1024,1,1,1,1]{0,4,3,2,1:T(1,128)S(1)}, /*i...) while((s32[]{:T(128)}, ...), condition=%wide.region_6.7_spmd.clone, body=%wide.region_3.6_spmd.clone.sunk | while | flops 181486592 | bytes 8243435 | solution.py:102
  80.4 2.2 select_reduce_fusion.8
  82.6 1.5 fusion.49
  84.1 1.6 fusion.50
  90.6 2.2 select_reduce_fusion.8
  92.8 1.5 fusion.49
  94.3 1.6 fusion.50
  98.3 2.3 %reduce.6 = bf16[1024,80]{1,0:T(8,128)(2,1)S(1)} reduce(bf16[1024,1,80]{2,1,0:T(2,128)(2,1)S(1)} %reshape.474, bf16[]{:T(256)} %broadcast.483), dimensions={1}, to_apply=%reshape.474.reduce_sub_computation | reduce | bytes 327682 | tf_op jit(solution)/shard_map/transpose;reshape;transpose | solution.py:160
  101.0 12.5 %all_to_all.69 = bf16[16,2,2560]{2,1,0:T(2,128)(2,1)S(1)} all-to-all(bf16[16,2,2560]{2,1,0:T(2,128)(2,1)S(1)} %reshape.477), channel_id=1, replica_groups=mesh['rows'=32,'seq'=16] {'seq'}, dimensions={0} | all-to-all | bytes 327680 | tf_op jit(solution)/shard_map/all_to_all | solution.py:161
  115.5 2.7 %fusion.37 = (f32[64]{0:T(128)S(1)}, f32[64,1280]{1,0:T(8,128)S(1)}) fusion(bf16[64,1280]{1,0:T(8,128)(2,1)S(1)} %reshape.466, bf16[1280,1280]{1,0:T(8,128)(2,1)} %all-gather.3.cloned.1.call-done, bf16[1,64,1280]{2,1,0:T(8,128)(2,1)S(1)} %copy-done.1), kind=kOutput, calls=%fused_computation.105 | convolution fusion | flops 209960896 | bytes 3932416 | tf_op jit(solution)/shard_map/dot_general | solution.py:163
  123.7 36.8 %all-gather.5.cloned.1.call-done = bf16[256,5120]{1,0:T(8,128)(2,1)} async-done(((bf16[16,5120]{1,0:T(8,128)(2,1)}), bf16[256,5120]{1,0:T(8,128)(2,1)}) %all-gather.5.cloned.1.call-update) | async-done | bytes 2621456 | tf_op jit(solution)/shard_map/all_gather | solution.py:172
  160.5 2.9 %fusion.36 = (f32[256]{0:T(256)S(1)}, f32[256]{0:T(256)S(1)}) fusion(bf16[256,5120]{1,0:T(8,128)(2,1)} %all-gather.5.cloned.1.call-done, bf16[5120,256]{1,0:T(8,128)(2,1)S(1)} %copy-done), kind=kOutput, calls=%fused_computation.104 | convolution fusion | flops 671284736 | bytes 5244928 | tf_op jit(solution)/shard_map/dot_general | solution.py:171
  163.5 23.2 %pmax.7 = f32[16]{0:T(128)S(1)} all-reduce(f32[16]{0:T(128)S(1)} %get-tuple-element.96), channel_id=1, replica_groups=mesh['rows'=32,'seq'=16] {'seq'}, use_global_device_ids=true, to_apply=%region_17.18 | all-reduce | flops 16 | bytes 128 | tf_op jit(solution)/shard_map/pmax | solution.py:192
  187.4 25.2 %all-reduce = f32[16]{0:T(128)S(1)} all-reduce(f32[16]{0:T(128)S(1)} %get-tuple-element.97), channel_id=2, replica_groups=mesh['rows'=32,'seq'=16] {'seq'}, use_global_device_ids=true, to_apply=%region_14.15.clone | all-reduce | flops 16 | bytes 128
  (83 shorter events, 28.3 us)
Async XLA Ops:
  7.2 153.3 %copy-start = (bf16[5120,256]{1,0:T(8,128)(2,1)S(1)}, bf16[5120,256]{1,0:T(8,128)(2,1)}, u32[]{:S(2)}) copy-start(bf16[5120,256]{1,0:T(8,128)(2,1)} %param.21) | copy-start | bytes 7864324
  8.6 21.6 %all-to-all-start = ((s32[64,1,16,1,1]{0,4,3,1,2:T(1,128)}), s32[64,1,16,1,1]{0,4,3,1,2:T(1,128)S(1)}, u32[]{:S(2)}, u32[]{:S(2)}) async-start(s32[64,1,16,1,1]{0,4,3,1,2:T(1,128)} %broadcast_in_dim.146), calls=%async_computation | async-start | bytes 16384 | tf_op jit(solution)/shard_map/all_to_all | solution.py:150
  18.7 96.8 %all-gather.3.cloned.1.call-start = ((), (), s32[]{:S(2)}) async-start(), calls=%async_computation.4 | async-start | bytes 3379200 | tf_op jit(solution)/shard_map/all_gather | solution.py:165
  28.0 2.2 copy-start.6
  30.8 14.2 %all-to-all-start.1 = ((s32[64,1,16,1,1]{0,4,3,1,2:T(1,128)}), s32[64,1,16,1,1]{0,4,3,1,2:T(1,128)S(1)}, u32[]{:S(2)}, u32[]{:S(2)}) async-start(s32[64,1,16,1,1]{0,4,3,1,2:T(1,128)} %broadcast_in_dim.148), calls=%async_computation.1 | async-start | bytes 16384 | tf_op jit(solution)/shard_map/all_to_all | solution.py:151
  45.0 26.8 %all-to-all-start.2 = ((bf16[64,3,16,1,80]{4,0,1,3,2:T(8,128)(2,1)}), bf16[64,3,16,1,80]{4,0,1,3,2:T(8,128)(2,1)S(1)}, u32[]{:S(2)}, u32[]{:S(2)}) async-start(bf16[64,3,16,1,80]{4,0,1,3,2:T(8,128)(2,1)} %copy.49), calls=%async_computation.2 | async-start | bytes 1572864 | tf_op jit(solution)/shard_map/all_to_all | solution.py:149
  49.1 111.4 %all-gather.5.cloned.1.call-start = ((), (), s32[]{:S(2)}) async-start(), calls=%async_computation.5 | async-start | bytes 2785280 | tf_op jit(solution)/shard_map/all_gather | solution.py:172
  82.6 1.5 copy-start.2
  85.7 0.7 copy-start.3
  92.8 1.5 copy-start.2
  95.8 0.7 copy-start.3
  101.0 14.5 %copy-start.1 = (bf16[1,64,1280]{2,1,0:T(8,128)(2,1)S(1)}, bf16[1,64,1280]{2,1,0:T(8,128)(2,1)}, u32[]{:S(2)}) copy-start(bf16[1,64,1280]{2,1,0:T(8,128)(2,1)} %param.13) | copy-start | bytes 491524
  115.4 3.0 %copy-start.4 = (f32[1280]{0:T(1024)S(1)}, f32[1280]{0:T(1024)}, u32[]{:S(2)}) copy-start(f32[1280]{0:T(1024)} %param.20) | copy-start | bytes 15364
  115.4 3.0 %copy-start.5 = (f32[1280]{0:T(1024)S(1)}, f32[1280]{0:T(1024)}, u32[]{:S(2)}) copy-start(f32[1280]{0:T(1024)} %param.19) | copy-start | bytes 15364
  115.5 4.0 %copy-start.7 = (s32[1,4]{1,0:T(1,128)S(1)}, s32[1,4]{1,0:T(1,128)}, u32[]{:S(2)}) copy-start(s32[1,4]{1,0:T(1,128)} %param.17) | copy-start | bytes 52
  115.5 4.0 %copy-start.8 = (s32[4]{0:T(128)S(1)}, s32[4]{0:T(128)}, u32[]{:S(2)}) copy-start(s32[4]{0:T(128)} %get-tuple-element.120) | copy-start | bytes 52
Sparse Core Ops, SparseCore 0:
  22.7 84.2 all-gather.2
  119.5 40.9 all-gather.4
where the time goes:
time: 225 us; the launch traced here: 224 us
  waiting for transfers between devices  63.9 us (28%)
  blocking collectives  61 us (27%)
  local copies, waits for them, and re-layouts  22.6 us (10%)
  starting transfers between devices  21.5 us (10%)
  between operations  19.3 us (9%)
  other arithmetic  18.7 us (8%)
  matrix products  13.1 us (6%)
  loops' own time  4.26 us (2%)
    all_gather x1, waiting for transfers between devices, body(): lax.all_gather(merged, 'seq', axis=0, tiled=True)  36.8 us
    unnamed x1, blocking collectives  25.2 us
    pmax x1, blocking collectives, body(): lax.pmax(tops_all, 'seq')  23.2 us
    all_to_all x1, waiting for transfers between devices, body(): lax.all_to_all(packed, 'seq', split_axis=2, concat_axis=0, tiled=True)  22 us
    all_to_all x1, blocking collectives, body(): lax.all_to_all(head_out, 'seq', split_axis=0, concat_axis=1, tiled=True)  12.5 us
    all_to_all x1, starting transfers between devices, body(): lax.all_to_all(segment_tile, 'seq', split_axis=2, concat_axis=0, tiled=True)  10.1 us
    all_to_all x1, starting transfers between devices, body(): lax.all_to_all(keep_tile, 'seq', split_axis=2, concat_axis=0, tiled=True)  7.27 us
  transfers between devices with their start and end apart: 5, of which 3 were waited for; matrix products, arithmetic and copies ran while one was open for 18% of the time, Pallas kernels for 0%

commit v1 on v0

--- a/solution.py
+++ b/solution.py
@@ -7,6 +7,13 @@
 HD = 80
 OUT = 4096
 SLOT_DEV = 1
+
+
+def all_by_exchange(x, axis, along):
+    count = lax.axis_size(axis)
+    tiles = jnp.stack([x for _ in range(count)])
+    tiles = lax.all_to_all(tiles, axis, split_axis=0, concat_axis=0)
+    return jnp.concatenate(tiles, axis=along)
 
 
 def positions(segment, places, patch_grid):
@@ -169,9 +176,7 @@
     normed = layer_norm(mixed, norm_gain, norm_bias)
     merged = normed.reshape(tok_count // 4, 4 * normed.shape[1])
     projected = jnp.dot(
-        lax.all_gather(merged, "seq", axis=0, tiled=True),
-        merge_weight,
-        preferred_element_type=jnp.float32,
+        all_by_exchange(merged, "seq", 0), merge_weight, preferred_element_type=jnp.float32
     )
     merge_stats = jnp.stack([jnp.sum(projected * projected, axis=1), jnp.max(projected, axis=1)])
     slot_total = SLOT_DEV * seq_count

time: 225 us -> 248 us (1.10)
  waiting for transfers between devices: 63.9 us -> 83 us
  starting transfers between devices: 21.5 us -> 25.9 us
    all_to_all x0 -> x1, waiting for transfers between devices: none -> 55.4 us  [all_by_exchange(): tiles = lax.all_to_all(tiles, axis, split_axis=0, concat_axis=0)]
    all_gather x1 -> x0, waiting for transfers between devices: 36.8 us -> none  [body(): lax.all_gather(merged, 'seq', axis=0, tiled=True)]
    all_to_all x0 -> x1, starting transfers between devices: none -> 4.48 us  [all_by_exchange(): tiles = lax.all_to_all(tiles, axis, split_axis=0, concat_axis=0)]
  transfers between devices with their start and end apart: 5 -> 5, of which waited for: 3 -> 3; matrix products, arithmetic and copies ran while one was open for 18% -> 16% of each run, Pallas kernels for 0% -> 0%
where the time goes in v1:
time: 248 us; the launch traced here: 247 us
  waiting for transfers between devices  83 us (33%)
  blocking collectives  60.5 us (24%)
  starting transfers between devices  25.9 us (10%)
  local copies, waits for them, and re-layouts  22.4 us (9%)
  between operations  19.2 us (8%)
  other arithmetic  18.2 us (7%)
  matrix products  13.2 us (5%)
  loops' own time  4.25 us (2%)
    all_to_all x1, waiting for transfers between devices, all_by_exchange(): tiles = lax.all_to_all(tiles, axis, split_axis=0, concat_axis=0)  55.4 us
    pmax x1, blocking collectives, body(): lax.pmax(tops_all, 'seq')  24.1 us
    unnamed x1, blocking collectives  23.9 us
    all_to_all x1, waiting for transfers between devices, body(): lax.all_to_all(packed, 'seq', split_axis=2, concat_axis=0, tiled=True)  22.5 us
    all_to_all x1, blocking collectives, body(): lax.all_to_all(head_out, 'seq', split_axis=0, concat_axis=1, tiled=True)  12.5 us
    all_to_all x1, starting transfers between devices, body(): lax.all_to_all(segment_tile, 'seq', split_axis=2, concat_axis=0, tiled=True)  10.1 us
    all_to_all x1, starting transfers between devices, body(): lax.all_to_all(keep_tile, 'seq', split_axis=2, concat_axis=0, tiled=True)  7.27 us
  transfers between devices with their start and end apart: 5, of which 3 were waited for; matrix products, arithmetic and copies ran while one was open for 16% of the time, Pallas kernels for 0%

profile of v1, /device:TPU:1, one launch (start us, length us, event | category | flops | bytes accessed | tf_op | source)
XLA Modules:
  0.0 246.7 jit_solution(313945075450464884)
XLA Ops:
  8.6 10.1 %all-to-all-start = ((s32[64,1,16,1,1]{0,4,3,1,2:T(1,128)}), s32[64,1,16,1,1]{0,4,3,1,2:T(1,128)S(1)}, u32[]{:S(2)}, u32[]{:S(2)}) async-start(s32[64,1,16,1,1]{0,4,3,1,2:T(1,128)} %broadcast_in_dim.146), calls=%async_computation | async-start | bytes 16384 | tf_op jit(solution)/shard_map/all_to_all | solution.py:157
  19.4 2.4 reshape_squeeze.3
  30.8 7.3 %all-to-all-start.1 = ((s32[64,1,16,1,1]{0,4,3,1,2:T(1,128)}), s32[64,1,16,1,1]{0,4,3,1,2:T(1,128)S(1)}, u32[]{:S(2)}, u32[]{:S(2)}) async-start(s32[64,1,16,1,1]{0,4,3,1,2:T(1,128)} %broadcast_in_dim.148), calls=%async_computation.1 | async-start | bytes 16384 | tf_op jit(solution)/shard_map/all_to_all | solution.py:158
  38.1 1.5 maximum_bitcast_fusion
  40.7 4.3 %all-to-all-done.1 = s32[64,1,16,1,1]{0,4,3,1,2:T(1,128)S(1)} async-done(((s32[64,1,16,1,1]{0,4,3,1,2:T(1,128)}), s32[64,1,16,1,1]{0,4,3,1,2:T(1,128)S(1)}, u32[]{:S(2)}, u32[]{:S(2)}) %all-to-all-start.1) | async-done | bytes 4128 | tf_op jit(solution)/shard_map/all_to_all | solution.py:158
  45.0 4.1 %all-to-all-start.2 = ((bf16[64,3,16,1,80]{4,0,1,3,2:T(8,128)(2,1)}), bf16[64,3,16,1,80]{4,0,1,3,2:T(8,128)(2,1)S(1)}, u32[]{:S(2)}, u32[]{:S(2)}) async-start(bf16[64,3,16,1,80]{4,0,1,3,2:T(8,128)(2,1)} %copy.49), calls=%async_computation.2 | async-start | bytes 1572864 | tf_op jit(solution)/shard_map/all_to_all | solution.py:156
  49.3 22.5 %all-to-all-done.2 = bf16[64,3,16,1,80]{4,0,1,3,2:T(8,128)(2,1)S(1)} async-done(((bf16[64,3,16,1,80]{4,0,1,3,2:T(8,128)(2,1)}), bf16[64,3,16,1,80]{4,0,1,3,2:T(8,128)(2,1)S(1)}, u32[]{:S(2)}, u32[]{:S(2)}) %all-to-all-start.2) | async-done | bytes 491552 | tf_op jit(solution)/shard_map/all_to_all | solution.py:156
  73.3 1.9 all_to_all.64
  76.2 19.0 %while.11 = (s32[]{:T(128)}, bf16[2,1,512,80]{2,3,1,0:T(8,128)(2,1)}, s32[2]{0:T(128)S(1)}, s32[1024]{0:T(1024)S(1)}, s32[1024,1,1,1,1]{0,4,3,2,1:T(1,128)S(1)},...) while((s32[]{:T(128)}, ...), condition=%wide.region_6.7_spmd.clone, body=%wide.region_3.6_spmd.clone.sunk | while | flops 181486592 | bytes 8243443 | solution.py:109
  79.8 2.2 select_reduce_fusion.8
  82.0 1.5 fusion.49
  83.5 1.6 fusion.50
  89.3 2.2 select_reduce_fusion.8
  91.5 1.5 fusion.49
  93.0 1.6 fusion.50
  97.0 2.3 reduce.6
  99.8 12.5 %all_to_all.74 = bf16[16,2,2560]{2,1,0:T(2,128)(2,1)S(1)} all-to-all(bf16[16,2,2560]{2,1,0:T(2,128)(2,1)S(1)} %reshape.479), channel_id=1, replica_groups=mesh['rows'=32,'seq'=16] {'seq'}, dimensions={0} | all-to-all | bytes 327680 | tf_op jit(solution)/shard_map/all_to_all | solution.py:168
  114.2 2.7 %fusion.37 = (f32[64]{0:T(128)S(1)}, f32[64,1280]{1,0:T(8,128)S(1)}) fusion(bf16[64,1280]{1,0:T(8,128)(2,1)S(1)} %reshape.468, bf16[1280,1280]{1,0:T(8,128)(2,1)} %all-gather.2.cloned.1.call-done, bf16[1,64,1280]{2,1,0:T(8,128)(2,1)S(1)} %copy-done.1), kind=kOutput, calls=%fused_computation.105 | convolution fusion | flops 209960896 | bytes 3932416 | tf_op jit(solution)/shard_map/dot_general | solution.py:170
  117.4 1.8 stack.9
  119.2 4.5 %all-to-all-start.4 = ((bf16[16,16,5120]{2,1,0:T(8,128)(2,1)}), bf16[16,16,5120]{2,1,0:T(8,128)(2,1)}, u32[]{:S(2)}, u32[]{:S(2)}) async-start(bf16[16,16,5120]{2,1,0:T(8,128)(2,1)} %stack.9), calls=%async_computation.4 | async-start | bytes 5242880 | tf_op jit(solution)/shard_map/all_to_all | solution.py:15
  128.0 55.4 %all-to-all-done.4 = bf16[16,16,5120]{2,1,0:T(8,128)(2,1)} async-done(((bf16[16,16,5120]{2,1,0:T(8,128)(2,1)}), bf16[16,16,5120]{2,1,0:T(8,128)(2,1)}, u32[]{:S(2)}, u32[]{:S(2)}) %all-to-all-start.4) | async-done | bytes 2621472 | tf_op jit(solution)/shard_map/all_to_all | solution.py:15
  183.4 2.9 %fusion.36 = (f32[256]{0:T(256)S(1)}, f32[256]{0:T(256)S(1)}) fusion(bf16[256,5120]{1,0:T(8,128)(2,1)} %bitcast.38, bf16[5120,256]{1,0:T(8,128)(2,1)S(1)} %copy-done), kind=kOutput, calls=%fused_computation.104 | convolution fusion | flops 671284736 | bytes 5244928 | tf_op jit(solution)/shard_map/dot_general | solution.py:178
  186.4 23.9 %all-reduce = f32[16]{0:T(128)S(1)} all-reduce(f32[16]{0:T(128)S(1)} %get-tuple-element.97), channel_id=2, replica_groups=mesh['rows'=32,'seq'=16] {'seq'}, use_global_device_ids=true, to_apply=%region_14.15.clone | all-reduce | flops 16 | bytes 128
  212.3 24.1 %pmax.7 = f32[16]{0:T(128)S(1)} all-reduce(f32[16]{0:T(128)S(1)} %get-tuple-element.96), channel_id=1, replica_groups=mesh['rows'=32,'seq'=16] {'seq'}, use_global_device_ids=true, to_apply=%region_17.18 | all-reduce | flops 16 | bytes 128 | tf_op jit(solution)/shard_map/pmax | solution.py:197
  (87 shorter events, 28.5 us)
Async XLA Ops:
  7.2 176.2 %copy-start = (bf16[5120,256]{1,0:T(8,128)(2,1)S(1)}, bf16[5120,256]{1,0:T(8,128)(2,1)}, u32[]{:S(2)}) copy-start(bf16[5120,256]{1,0:T(8,128)(2,1)} %param.21) | copy-start | bytes 7864324
  8.6 21.6 %all-to-all-start = ((s32[64,1,16,1,1]{0,4,3,1,2:T(1,128)}), s32[64,1,16,1,1]{0,4,3,1,2:T(1,128)S(1)}, u32[]{:S(2)}, u32[]{:S(2)}) async-start(s32[64,1,16,1,1]{0,4,3,1,2:T(1,128)} %broadcast_in_dim.146), calls=%async_computation | async-start | bytes 16384 | tf_op jit(solution)/shard_map/all_to_all | solution.py:157
  18.7 95.5 %all-gather.2.cloned.1.call-start = ((), (), s32[]{:S(2)}) async-start(), calls=%async_computation.5 | async-start | bytes 3379200 | tf_op jit(solution)/shard_map/all_gather | solution.py:172
  23.3 5.4 %copy-start.6 = (s32[4,1]{0,1:T(1,128)}, s32[4,1]{0,1:T(1,128)S(1)}, u32[]{:S(2)}) copy-start(s32[4,1]{0,1:T(1,128)S(1)} %reduce-window.7) | copy-start | bytes 52
  28.7 1.5 copy-start.8
  30.8 14.2 %all-to-all-start.1 = ((s32[64,1,16,1,1]{0,4,3,1,2:T(1,128)}), s32[64,1,16,1,1]{0,4,3,1,2:T(1,128)S(1)}, u32[]{:S(2)}, u32[]{:S(2)}) async-start(s32[64,1,16,1,1]{0,4,3,1,2:T(1,128)} %broadcast_in_dim.148), calls=%async_computation.1 | async-start | bytes 16384 | tf_op jit(solution)/shard_map/all_to_all | solution.py:158
  45.0 26.8 %all-to-all-start.2 = ((bf16[64,3,16,1,80]{4,0,1,3,2:T(8,128)(2,1)}), bf16[64,3,16,1,80]{4,0,1,3,2:T(8,128)(2,1)S(1)}, u32[]{:S(2)}, u32[]{:S(2)}) async-start(bf16[64,3,16,1,80]{4,0,1,3,2:T(8,128)(2,1)} %copy.49), calls=%async_computation.2 | async-start | bytes 1572864 | tf_op jit(solution)/shard_map/all_to_all | solution.py:156
  82.0 1.5 copy-start.2
  85.1 0.7 copy-start.3
  91.5 1.5 copy-start.2
  94.6 0.7 copy-start.3
  99.7 14.4 %copy-start.1 = (bf16[1,64,1280]{2,1,0:T(8,128)(2,1)S(1)}, bf16[1,64,1280]{2,1,0:T(8,128)(2,1)}, u32[]{:S(2)}) copy-start(bf16[1,64,1280]{2,1,0:T(8,128)(2,1)} %param.13) | copy-start | bytes 491524
  114.1 3.0 %copy-start.4 = (f32[1280]{0:T(1024)S(1)}, f32[1280]{0:T(1024)}, u32[]{:S(2)}) copy-start(f32[1280]{0:T(1024)} %param.20) | copy-start | bytes 15364
  114.1 3.0 %copy-start.5 = (f32[1280]{0:T(1024)S(1)}, f32[1280]{0:T(1024)}, u32[]{:S(2)}) copy-start(f32[1280]{0:T(1024)} %param.19) | copy-start | bytes 15364
  119.2 4.5 %copy-start.9 = (s32[1,4]{1,0:T(1,128)S(1)}, s32[1,4]{1,0:T(1,128)}, u32[]{:S(2)}) copy-start(s32[1,4]{1,0:T(1,128)} %param.17) | copy-start | bytes 52
  119.2 4.5 %copy-start.10 = (s32[4]{0:T(128)S(1)}, s32[4]{0:T(128)}, u32[]{:S(2)}) copy-start(s32[4]{0:T(128)} %get-tuple-element.120) | copy-start | bytes 52
  119.2 7.8 %copy-start.7 = (s32[4,1]{0,1:T(1,128)S(1)}, s32[4,1]{0,1:T(1,128)}, u32[]{:S(2)}) copy-start(s32[4,1]{0,1:T(1,128)} %copy-done.6) | copy-start | bytes 52
  119.2 64.2 %all-to-all-start.4 = ((bf16[16,16,5120]{2,1,0:T(8,128)(2,1)}), bf16[16,16,5120]{2,1,0:T(8,128)(2,1)}, u32[]{:S(2)}, u32[]{:S(2)}) async-start(bf16[16,16,5120]{2,1,0:T(8,128)(2,1)} %stack.9), calls=%async_computation.4 | async-start | bytes 5242880 | tf_op jit(solution)/shard_map/all_to_all | solution.py:15
Sparse Core Ops, SparseCore 0:
  22.7 84.2 all-gather.1
